TPU v7x, 32 devices: a whole 2x2x4 slice. The times are simulated.
32 devices in a mesh: parts: 2 (over x), loop: 4 (over y, core), tgrp: 4 (over z).
Axes of the slice: x: 2, y: 2, z: 4, core: 2. Of those that a mesh axis runs over, the one named last changes fastest.
Arguments:
- data: bfloat16 [8, 3, 12288], P(('parts', 'loop'), None, 'tgrp'), parts along dimension 0
- templates: bfloat16 [128, 4, 3, 2048], P('tgrp', 'loop')
- masks: int32 [128, 4], replicated, may hold values from 0 to 1, as said below
- offsets: int32 [8], P(('parts', 'loop')), parts along dimension 0, may hold values from 0 to 512, as said below
- active: int32 [8, 3], P(('parts', 'loop')), parts along dimension 0, may hold values 0 or 1
Outputs:
- detection: float32 [256, 12288], P(('parts', 'loop'), 'tgrp'), parts along dimension 0
There are 2 independent parts, one for each index of `parts`. A program takes and returns all parts, laid end to end along the dimension named above; an argument that names none is the same for every part. Nothing has to cross between parts.
Inputs may be any that keep to these rules, and one draw needn't show every extreme that they name: `masks`: every template uses at least one station. `offsets`: some station has an offset of exactly 512.
All inputs are finite; a program needn't handle non-finite values. No bound on the sum of `active` on one device may be relied on, other than what follows from the above.
Results may differ from a plain program's by a relative error of at most 0.0003.
Values may be sent and summed in bfloat16 or wider, within the bound.
No kernel may reach another device: no remote copies, remote signals or barrier semaphores. Data moves between devices by JAX's collectives and lax.ppermute only.
A program may use at most 64 MiB of HBM per device.

v0:
```python
import jax
import jax.numpy as jnp
from jax import lax
from jax.sharding import PartitionSpec as P

L = 2048
epsilon = 1e-05


def passed_along(value, axis, steps):
    count = lax.axis_size(axis)
    initial, last = (max(0, -steps), min(count, count - steps))
    return lax.ppermute(value, axis, [(source, source + steps) for source in range(initial, last)])


def window_energy(squares, out_len, span):
    inner_len = out_len + span - 128
    nblocks = (inner_len + 127) // 128
    total_len = 128 * (nblocks + 1)
    padded = jnp.concatenate([squares, jnp.zeros((total_len - squares.shape[0],), squares.dtype)])
    first = padded[: 128 * nblocks].reshape(nblocks, 128)
    second = padded[128 : 128 * nblocks + 128].reshape(nblocks, 128)
    segments = jnp.concatenate([first, second], axis=1)
    rows_at = lax.broadcasted_iota(jnp.int32, (256, 128), 0)
    cols_at = lax.broadcasted_iota(jnp.int32, (256, 128), 1)
    gap = rows_at - cols_at
    band = jnp.where((gap >= 0) & (gap < 128), 1.0, 0.0).astype(squares.dtype)
    inner = jnp.dot(segments, band, precision=lax.Precision.HIGHEST).reshape(nblocks * 128)
    energy = jnp.zeros((out_len,), squares.dtype)
    for block_at in range(span // 128):
        energy = energy + inner[128 * block_at : 128 * block_at + out_len]
    return energy


def correlate(panel, window, out_len):
    row_count = panel.shape[0]
    blocks = panel.shape[2] // 128
    span_len = out_len + panel.shape[2] - 128
    unfold = jnp.stack(
        [window[:, shift_by : shift_by + span_len] for shift_by in range(128)], axis=1
    )
    unfold = unfold.reshape(3 * 128, span_len)
    frames = (
        panel.reshape(row_count, 3, blocks, 128)
        .transpose(0, 2, 1, 3)
        .reshape(row_count, blocks, 3 * 128)
    )

    def add_block(block_at, running_sum):
        start_at = (block_at * 128).astype(jnp.int32)
        columns = lax.dynamic_slice_in_dim(unfold, start_at, out_len, 1)
        weights_now = lax.dynamic_index_in_dim(frames, block_at, 1, keepdims=False)
        return running_sum + jnp.dot(weights_now, columns, preferred_element_type=jnp.float32)

    return lax.fori_loop(0, blocks, add_block, jnp.zeros((row_count, out_len), jnp.float32))


def local(data, templates, masks, offsets, active):
    local_count = data.shape[0]
    block_len = data.shape[2]
    following = passed_along(data, "tgrp", -1)
    extended = jnp.concatenate([data, following], axis=2)
    loop_at = lax.axis_index("loop")
    first_station = loop_at * local_count
    counts = jnp.sum(masks, axis=1).astype(jnp.float32)
    local_masks = lax.dynamic_slice_in_dim(masks, first_station, local_count, 1)
    weights = local_masks.astype(jnp.float32) * jnp.sqrt(3.0 * L / counts)[:, None]
    station = 0
    channel_on = active[station].astype(jnp.bfloat16)
    series = lax.dynamic_slice(
        extended[station], (jnp.int32(0), offsets[station]), (3, block_len + L)
    )
    window = series * channel_on[:, None]
    wide_window = window.astype(jnp.float32)
    squares = jnp.sum(wide_window * wide_window, axis=0)
    energy = window_energy(squares, block_len, L)
    inv_datas = [1.0 / jnp.sqrt(energy / (3.0 * L) + epsilon)]
    windows = [window]
    channel_sets = [channel_on]
    panel_rows = lax.all_gather(templates, "tgrp", axis=0, tiled=True)
    station = 0
    panel = panel_rows[:, station] * channel_sets[station][None, :, None]
    wide_panel = panel.astype(jnp.float32)
    inv_template = 1.0 / jnp.sqrt(
        jnp.sum(wide_panel * wide_panel, axis=(1, 2)) / (3.0 * L) + epsilon
    )
    corr = correlate(panel, windows[station], block_len)
    row_weights = weights[:, station]
    row_scale = inv_template * row_weights
    stacked = corr * inv_datas[station][None, :] * row_scale[:, None] / (3.0 * L)
    rows_here = stacked.shape[0] // lax.axis_size("loop")
    summed = lax.psum(stacked, "loop")
    return lax.dynamic_slice_in_dim(summed, loop_at * rows_here, rows_here, 0)


def solution(mesh):
    placed = (
        P(("parts", "loop"), None, "tgrp"),
        P("tgrp", "loop", None, None),
        P(),
        P(("parts", "loop")),
        P(("parts", "loop"), None),
    )
    return jax.shard_map(
        local, mesh=mesh, in_specs=placed, out_specs=P(("parts", "loop"), "tgrp"), check_vma=False
    )
```

profile of v0, /device:TPU:0, one launch (start us, length us, event | category | flops | bytes accessed | tf_op | source)
XLA Modules:
  0.0 146.2 jit_solution(8335573352305815033)
XLA Ops:
  6.5 1.3 collective-permute-start
  7.9 0.7 convert_bitcast_fusion
  9.2 0.7 reduce_sum.29
  9.9 3.5 %collective-permute-done = bf16[1,3,3072]{2,1,0:T(4,128)(2,1)S(1)} collective-permute-done((bf16[1,3,3072]{2,1,0:T(4,128)(2,1)}, bf16[1,3,3072]{2,1,0:T(4,128)(2,1)S(1)}, u32[]{:S(2)}, u32[]{:S(2)}) %collective-permute-start) | collective-permute-done | bytes 18464 | tf_op jit(solution)/shard_map/ppermute | solution.py:13
  13.5 0.9 multiply_reduce_fusion.1
  14.4 0.1 constant_dynamic-update-slice_fusion.126
  14.9 0.1 constant_dynamic-update-slice_fusion.122
  15.0 0.1 constant_dynamic-update-slice_fusion.121
  15.1 0.1 constant_dynamic-update-slice_fusion.120
  15.3 0.1 constant_dynamic-update-slice_fusion.118
  15.4 0.1 constant_dynamic-update-slice_fusion.117
  15.9 0.1 constant_dynamic-update-slice_fusion.112
  16.1 0.1 constant_dynamic-update-slice_fusion.111
  16.4 0.1 constant_dynamic-update-slice_fusion.108
  16.8 0.1 constant_dynamic-update-slice_fusion.104
  16.9 0.1 constant_dynamic-update-slice_fusion.103
  17.7 0.1 constant_dynamic-update-slice_fusion.96
  17.8 0.1 constant_dynamic-update-slice_fusion.95
  18.0 0.1 constant_dynamic-update-slice_fusion.93
  18.3 0.1 constant_dynamic-update-slice_fusion.90
  18.9 0.1 constant_dynamic-update-slice_fusion.85
  19.2 0.1 constant_dynamic-update-slice_fusion.82
  19.4 0.1 constant_dynamic-update-slice_fusion.80
  19.8 0.1 constant_dynamic-update-slice_fusion.76
  20.3 0.1 constant_dynamic-update-slice_fusion.72
  21.1 0.1 constant_dynamic-update-slice_fusion.64
  21.2 0.1 constant_dynamic-update-slice_fusion.63
  21.8 0.1 constant_dynamic-update-slice_fusion.58
  22.1 0.1 constant_dynamic-update-slice_fusion.55
  22.3 0.1 constant_dynamic-update-slice_fusion.53
  22.6 0.1 constant_dynamic-update-slice_fusion.50
  22.8 0.1 constant_dynamic-update-slice_fusion.48
  23.1 0.1 constant_dynamic-update-slice_fusion.46
  24.6 0.1 constant_dynamic-update-slice_fusion.32
  26.3 0.1 constant_dynamic-update-slice_fusion.16
  28.0 0.1 constant_dynamic-update-slice_fusion
  28.1 2.2 %copy.141 = bf16[3,128,4992]{2,1,0:T(8,128)(2,1)} copy(bf16[3,128,4992]{2,0,1:T(4,128)(2,1)S(1)} %constant_dynamic-update-slice_fusion) | data formatting | bytes 7667712 | tf_op jit(solution)/shard_map/stack | solution.py:39
  30.4 0.2 fusion.4
  30.6 18.2 %all-gather.2.cloned.1.call-done = bf16[128,1,3,2048]{3,0,2,1:T(8,128)(2,1)} async-done(((bf16[32,1,3,2048]{3,0,2,1:T(8,128)(2,1)}), bf16[128,1,3,2048]{3,0,2,1:T(8,128)(2,1)}) %all-gather.2.cloned.1.call-update) | async-done | bytes 1572880 | tf_op jit(solution)/shard_map/all_gather | solution.py:80
  48.9 1.9 %copy.139 = bf16[128,1,3,2048]{0,3,2,1:T(8,128)(2,1)S(1)} copy(bf16[128,1,3,2048]{3,0,2,1:T(8,128)(2,1)} %all-gather.2.cloned.1.call-done) | data formatting | bytes 3145728 | tf_op jit(solution)/shard_map/all_gather | solution.py:80
  50.8 0.2 multiply_bitcast_fusion
  51.0 1.3 copy.140
  52.3 40.8 %while.14 = (s32[]{:T(128)}, f32[128,3072]{1,0:T(8,128)S(1)}, bf16[128,16,384]{0,2,1:T(8,128)(2,1)}, bf16[384,4992]{1,0:T(8,128)(2,1)}, s32[]{:T(128)}, /*index=5*/s32[]{:T(128)}, s32[]{:T(128)}, s32[]{:T(128)}) while((s32[]{:T(128)}, f32[128,3072]{1,0:T(8,128)S(1)}, bf16[128,16,384]{0,2,1:T(8,128)(2,1)}, ...), condition=%wide.region_1.0_spmd.clone, body=%wide.region_0.0_spmd.clone.sunk | while | flops 302776320 | bytes 5603985 | solution.py:55
  52.3 2.6 %convolution_add_fusion.2 = f32[128,3072]{1,0:T(8,128)S(1)} fusion(bf16[384,4992]{1,0:T(8,128)(2,1)} %get-tuple-element.168, s32[]{:T(128)S(6)} %select_n.34, f32[128,3072]{1,0:T(8,128)S(1)} %get-tuple-element.158, pred[]{:T(512)S(6)} %compare.3, bf16[128,16,384]{0,2,1:T(8,128)(2,1)} %get-tuple-element.167, s32[]{:T(128)} %get-tuple-element.157), kind=kOutput, calls=%fused_computation.clone.1 | convolution fusion | flops 302776320 | bytes 5603845 | tf_op jit(solution)/shard_map/while/body/eval_jaxpr/dot_general | solution.py:53
  54.9 2.5 %convolution_add_fusion.2 = f32[128,3072]{1,0:T(8,128)S(1)} fusion(bf16[384,4992]{1,0:T(8,128)(2,1)} %get-tuple-element.168, s32[]{:T(128)S(6)} %select_n.34, f32[128,3072]{1,0:T(8,128)S(1)} %get-tuple-element.158, pred[]{:T(512)S(6)} %compare.3, bf16[128,16,384]{0,2,1:T(8,128)(2,1)} %get-tuple-element.167, s32[]{:T(128)} %get-tuple-element.157), kind=kOutput, calls=%fused_computation.clone.1 | convolution fusion | flops 302776320 | bytes 5603845 | tf_op jit(solution)/shard_map/while/body/eval_jaxpr/dot_general | solution.py:53
  57.5 2.5 %convolution_add_fusion.2 = f32[128,3072]{1,0:T(8,128)S(1)} fusion(bf16[384,4992]{1,0:T(8,128)(2,1)} %get-tuple-element.168, s32[]{:T(128)S(6)} %select_n.34, f32[128,3072]{1,0:T(8,128)S(1)} %get-tuple-element.158, pred[]{:T(512)S(6)} %compare.3, bf16[128,16,384]{0,2,1:T(8,128)(2,1)} %get-tuple-element.167, s32[]{:T(128)} %get-tuple-element.157), kind=kOutput, calls=%fused_computation.clone.1 | convolution fusion | flops 302776320 | bytes 5603845 | tf_op jit(solution)/shard_map/while/body/eval_jaxpr/dot_general | solution.py:53
  60.0 2.5 %convolution_add_fusion.2 = f32[128,3072]{1,0:T(8,128)S(1)} fusion(bf16[384,4992]{1,0:T(8,128)(2,1)} %get-tuple-element.168, s32[]{:T(128)S(6)} %select_n.34, f32[128,3072]{1,0:T(8,128)S(1)} %get-tuple-element.158, pred[]{:T(512)S(6)} %compare.3, bf16[128,16,384]{0,2,1:T(8,128)(2,1)} %get-tuple-element.167, s32[]{:T(128)} %get-tuple-element.157), kind=kOutput, calls=%fused_computation.clone.1 | convolution fusion | flops 302776320 | bytes 5603845 | tf_op jit(solution)/shard_map/while/body/eval_jaxpr/dot_general | solution.py:53
  62.6 2.5 %convolution_add_fusion.2 = f32[128,3072]{1,0:T(8,128)S(1)} fusion(bf16[384,4992]{1,0:T(8,128)(2,1)} %get-tuple-element.168, s32[]{:T(128)S(6)} %select_n.34, f32[128,3072]{1,0:T(8,128)S(1)} %get-tuple-element.158, pred[]{:T(512)S(6)} %compare.3, bf16[128,16,384]{0,2,1:T(8,128)(2,1)} %get-tuple-element.167, s32[]{:T(128)} %get-tuple-element.157), kind=kOutput, calls=%fused_computation.clone.1 | convolution fusion | flops 302776320 | bytes 5603845 | tf_op jit(solution)/shard_map/while/body/eval_jaxpr/dot_general | solution.py:53
  65.1 2.5 %convolution_add_fusion.2 = f32[128,3072]{1,0:T(8,128)S(1)} fusion(bf16[384,4992]{1,0:T(8,128)(2,1)} %get-tuple-element.168, s32[]{:T(128)S(6)} %select_n.34, f32[128,3072]{1,0:T(8,128)S(1)} %get-tuple-element.158, pred[]{:T(512)S(6)} %compare.3, bf16[128,16,384]{0,2,1:T(8,128)(2,1)} %get-tuple-element.167, s32[]{:T(128)} %get-tuple-element.157), kind=kOutput, calls=%fused_computation.clone.1 | convolution fusion | flops 302776320 | bytes 5603845 | tf_op jit(solution)/shard_map/while/body/eval_jaxpr/dot_general | solution.py:53
  67.7 2.5 %convolution_add_fusion.2 = f32[128,3072]{1,0:T(8,128)S(1)} fusion(bf16[384,4992]{1,0:T(8,128)(2,1)} %get-tuple-element.168, s32[]{:T(128)S(6)} %select_n.34, f32[128,3072]{1,0:T(8,128)S(1)} %get-tuple-element.158, pred[]{:T(512)S(6)} %compare.3, bf16[128,16,384]{0,2,1:T(8,128)(2,1)} %get-tuple-element.167, s32[]{:T(128)} %get-tuple-element.157), kind=kOutput, calls=%fused_computation.clone.1 | convolution fusion | flops 302776320 | bytes 5603845 | tf_op jit(solution)/shard_map/while/body/eval_jaxpr/dot_general | solution.py:53
  70.2 2.5 %convolution_add_fusion.2 = f32[128,3072]{1,0:T(8,128)S(1)} fusion(bf16[384,4992]{1,0:T(8,128)(2,1)} %get-tuple-element.168, s32[]{:T(128)S(6)} %select_n.34, f32[128,3072]{1,0:T(8,128)S(1)} %get-tuple-element.158, pred[]{:T(512)S(6)} %compare.3, bf16[128,16,384]{0,2,1:T(8,128)(2,1)} %get-tuple-element.167, s32[]{:T(128)} %get-tuple-element.157), kind=kOutput, calls=%fused_computation.clone.1 | convolution fusion | flops 302776320 | bytes 5603845 | tf_op jit(solution)/shard_map/while/body/eval_jaxpr/dot_general | solution.py:53
  72.7 2.5 %convolution_add_fusion.2 = f32[128,3072]{1,0:T(8,128)S(1)} fusion(bf16[384,4992]{1,0:T(8,128)(2,1)} %get-tuple-element.168, s32[]{:T(128)S(6)} %select_n.34, f32[128,3072]{1,0:T(8,128)S(1)} %get-tuple-element.158, pred[]{:T(512)S(6)} %compare.3, bf16[128,16,384]{0,2,1:T(8,128)(2,1)} %get-tuple-element.167, s32[]{:T(128)} %get-tuple-element.157), kind=kOutput, calls=%fused_computation.clone.1 | convolution fusion | flops 302776320 | bytes 5603845 | tf_op jit(solution)/shard_map/while/body/eval_jaxpr/dot_general | solution.py:53
  75.3 2.5 %convolution_add_fusion.2 = f32[128,3072]{1,0:T(8,128)S(1)} fusion(bf16[384,4992]{1,0:T(8,128)(2,1)} %get-tuple-element.168, s32[]{:T(128)S(6)} %select_n.34, f32[128,3072]{1,0:T(8,128)S(1)} %get-tuple-element.158, pred[]{:T(512)S(6)} %compare.3, bf16[128,16,384]{0,2,1:T(8,128)(2,1)} %get-tuple-element.167, s32[]{:T(128)} %get-tuple-element.157), kind=kOutput, calls=%fused_computation.clone.1 | convolution fusion | flops 302776320 | bytes 5603845 | tf_op jit(solution)/shard_map/while/body/eval_jaxpr/dot_general | solution.py:53
  77.8 2.5 %convolution_add_fusion.2 = f32[128,3072]{1,0:T(8,128)S(1)} fusion(bf16[384,4992]{1,0:T(8,128)(2,1)} %get-tuple-element.168, s32[]{:T(128)S(6)} %select_n.34, f32[128,3072]{1,0:T(8,128)S(1)} %get-tuple-element.158, pred[]{:T(512)S(6)} %compare.3, bf16[128,16,384]{0,2,1:T(8,128)(2,1)} %get-tuple-element.167, s32[]{:T(128)} %get-tuple-element.157), kind=kOutput, calls=%fused_computation.clone.1 | convolution fusion | flops 302776320 | bytes 5603845 | tf_op jit(solution)/shard_map/while/body/eval_jaxpr/dot_general | solution.py:53
  80.4 2.5 %convolution_add_fusion.2 = f32[128,3072]{1,0:T(8,128)S(1)} fusion(bf16[384,4992]{1,0:T(8,128)(2,1)} %get-tuple-element.168, s32[]{:T(128)S(6)} %select_n.34, f32[128,3072]{1,0:T(8,128)S(1)} %get-tuple-element.158, pred[]{:T(512)S(6)} %compare.3, bf16[128,16,384]{0,2,1:T(8,128)(2,1)} %get-tuple-element.167, s32[]{:T(128)} %get-tuple-element.157), kind=kOutput, calls=%fused_computation.clone.1 | convolution fusion | flops 302776320 | bytes 5603845 | tf_op jit(solution)/shard_map/while/body/eval_jaxpr/dot_general | solution.py:53
  82.9 2.5 %convolution_add_fusion.2 = f32[128,3072]{1,0:T(8,128)S(1)} fusion(bf16[384,4992]{1,0:T(8,128)(2,1)} %get-tuple-element.168, s32[]{:T(128)S(6)} %select_n.34, f32[128,3072]{1,0:T(8,128)S(1)} %get-tuple-element.158, pred[]{:T(512)S(6)} %compare.3, bf16[128,16,384]{0,2,1:T(8,128)(2,1)} %get-tuple-element.167, s32[]{:T(128)} %get-tuple-element.157), kind=kOutput, calls=%fused_computation.clone.1 | convolution fusion | flops 302776320 | bytes 5603845 | tf_op jit(solution)/shard_map/while/body/eval_jaxpr/dot_general | solution.py:53
  85.5 2.5 %convolution_add_fusion.2 = f32[128,3072]{1,0:T(8,128)S(1)} fusion(bf16[384,4992]{1,0:T(8,128)(2,1)} %get-tuple-element.168, s32[]{:T(128)S(6)} %select_n.34, f32[128,3072]{1,0:T(8,128)S(1)} %get-tuple-element.158, pred[]{:T(512)S(6)} %compare.3, bf16[128,16,384]{0,2,1:T(8,128)(2,1)} %get-tuple-element.167, s32[]{:T(128)} %get-tuple-element.157), kind=kOutput, calls=%fused_computation.clone.1 | convolution fusion | flops 302776320 | bytes 5603845 | tf_op jit(solution)/shard_map/while/body/eval_jaxpr/dot_general | solution.py:53
  88.0 2.5 %convolution_add_fusion.2 = f32[128,3072]{1,0:T(8,128)S(1)} fusion(bf16[384,4992]{1,0:T(8,128)(2,1)} %get-tuple-element.168, s32[]{:T(128)S(6)} %select_n.34, f32[128,3072]{1,0:T(8,128)S(1)} %get-tuple-element.158, pred[]{:T(512)S(6)} %compare.3, bf16[128,16,384]{0,2,1:T(8,128)(2,1)} %get-tuple-element.167, s32[]{:T(128)} %get-tuple-element.157), kind=kOutput, calls=%fused_computation.clone.1 | convolution fusion | flops 302776320 | bytes 5603845 | tf_op jit(solution)/shard_map/while/body/eval_jaxpr/dot_general | solution.py:53
  90.5 2.5 %convolution_add_fusion.2 = f32[128,3072]{1,0:T(8,128)S(1)} fusion(bf16[384,4992]{1,0:T(8,128)(2,1)} %get-tuple-element.168, s32[]{:T(128)S(6)} %select_n.34, f32[128,3072]{1,0:T(8,128)S(1)} %get-tuple-element.158, pred[]{:T(512)S(6)} %compare.3, bf16[128,16,384]{0,2,1:T(8,128)(2,1)} %get-tuple-element.167, s32[]{:T(128)} %get-tuple-element.157), kind=kOutput, calls=%fused_computation.clone.1 | convolution fusion | flops 302776320 | bytes 5603845 | tf_op jit(solution)/shard_map/while/body/eval_jaxpr/dot_general | solution.py:53
  93.1 0.6 multiply_reduce_fusion
  93.6 0.7 fusion.29
  94.3 1.4 multiply_multiply_fusion
  95.8 41.9 %all-reduce.2.cloned.1.call-done = f32[128,3072]{1,0:T(8,128)} async-done(((f32[128,3072]{1,0:T(8,128)}), f32[128,3072]{1,0:T(8,128)}) %all-reduce.2.cloned.1.call-update) | async-done | bytes 1572880 | tf_op jit(solution)/shard_map/psum | solution.py:92
  137.6 1.8 %constant_dynamic-slice_fusion = f32[32,3072]{1,0:T(8,128)} fusion(f32[128,3072]{1,0:T(8,128)} %all-reduce.2.cloned.1.call-done, s32[]{:T(128)S(6)} %select_n.29), kind=kLoop, calls=%fused_computation.305 | loop fusion | bytes 786436 | tf_op jit(solution)/shard_map/dynamic_slice | solution.py:93
  (106 shorter events, 10.1 us)
Async XLA Ops:
  6.5 42.3 %all-gather.2.cloned.1.call-start = ((), (), s32[]{:S(2)}) async-start(), calls=%async_computation | async-start | bytes 1966080 | tf_op jit(solution)/shard_map/all_gather | solution.py:80
  6.5 6.9 %collective-permute-start = (bf16[1,3,3072]{2,1,0:T(4,128)(2,1)}, bf16[1,3,3072]{2,1,0:T(4,128)(2,1)S(1)}, u32[]{:S(2)}, u32[]{:S(2)}) collective-permute-start(bf16[1,3,3072]{2,1,0:T(4,128)(2,1)} %param.7), channel_id=1, source_target_pairs={{1,0},{2,1},{3,2},{5,4},{6,5},{7,6},{9,8},{10,9},{11,10},{13,12},{... | collective-permute-start | bytes 55304 | tf_op jit(solution)/shard_map/ppermute | solution.py:13
  7.8 129.8 %all-reduce.2.cloned.1.call-start = ((), (), s32[]{:S(2)}) async-start(), calls=%async_computation.1 | async-start | bytes 3145728 | tf_op jit(solution)/shard_map/psum | solution.py:92
  52.3 40.8 %copy-start = (bf16[128,1,3,2048]{3,0,2,1:T(8,128)(2,1)S(1)}, bf16[128,1,3,2048]{3,0,2,1:T(8,128)(2,1)}, u32[]{:S(2)}) copy-start(bf16[128,1,3,2048]{3,0,2,1:T(8,128)(2,1)} %all-gather.2.cloned.1.call-done) | copy-start | bytes 4718596
Sparse Core Ops, SparseCore 0:
  8.9 39.9 all-gather.1
  95.9 41.6 all-reduce.1
where the time goes:
time: 147 us; the launch traced here: 146 us
  waiting for transfers between devices  63.7 us (43%)
  matrix products  40.6 us (28%)
  local copies, waits for them, and re-layouts  20.5 us (14%)
  between operations  14.6 us (10%)
  other arithmetic  5.18 us (4%)
    psum x1, waiting for transfers between devices, local(): summed = lax.psum(stacked, 'loop')  41.9 us
    dot_general x16, matrix products, add_block(): jnp.dot(weights_now, columns, preferred_element_type=jnp.float32)  40.3 us
    all_gather x1, waiting for transfers between devices, local(): panel_rows = lax.all_gather(templates, 'tgrp', axis=0, tiled=True)  18.2 us
    unnamed x129, local copies, waits for them, and re-layouts  13.1 us
    ppermute x1, waiting for transfers between devices, passed_along(): lax.ppermute(value, axis, [(source, source + steps) for source in range(i...  3.55 us
  transfers between devices with their start and end apart: 3, of which 3 were waited for; matrix products, arithmetic and copies ran while one was open for 12% of the time, Pallas kernels for 0%

commit v1 on v0

--- a/solution.py
+++ b/solution.py
@@ -89,7 +89,8 @@
     row_scale = inv_template * row_weights
     stacked = corr * inv_datas[station][None, :] * row_scale[:, None] / (3.0 * L)
     rows_here = stacked.shape[0] // lax.axis_size("loop")
-    summed = lax.psum(stacked, "loop")
+    parts = lax.all_gather(stacked, "loop")
+    summed = jnp.sum(parts, axis=0)
     return lax.dynamic_slice_in_dim(summed, loop_at * rows_here, rows_here, 0)
 
 

time: 147 us -> 153 us (1.041)
  waiting for transfers between devices: 63.7 us -> 67.2 us
  other arithmetic: 5.18 us -> 8.57 us
    all_gather x0 -> x1, waiting for transfers between devices: none -> 45.4 us  [local(): parts = lax.all_gather(stacked, 'loop')]
    psum x1 -> x0, waiting for transfers between devices: 41.9 us -> none  [local(): summed = lax.psum(stacked, 'loop')]
    reduce_sum x0 -> x1, other arithmetic: none -> 3.39 us  [local(): summed = jnp.sum(parts, axis=0)]
where the time goes in v1:
time: 153 us; the launch traced here: 152 us
  waiting for transfers between devices  67.2 us (44%)
  matrix products  40.6 us (27%)
  local copies, waits for them, and re-layouts  19.5 us (13%)
  between operations  14.6 us (10%)
  other arithmetic  8.57 us (6%)
    all_gather x1, waiting for transfers between devices, local(): parts = lax.all_gather(stacked, 'loop')  45.4 us
    dot_general x16, matrix products, add_block(): jnp.dot(weights_now, columns, preferred_element_type=jnp.float32)  40.3 us
    all_gather x1, waiting for transfers between devices, local(): panel_rows = lax.all_gather(templates, 'tgrp', axis=0, tiled=True)  18.2 us
    unnamed x129, local copies, waits for them, and re-layouts  13.1 us
    ppermute x1, waiting for transfers between devices, passed_along(): lax.ppermute(value, axis, [(source, source + steps) for source in range(i...  3.55 us
    reduce_sum x1, other arithmetic, local(): summed = jnp.sum(parts, axis=0)  3.39 us
  transfers between devices with their start and end apart: 3, of which 3 were waited for; matrix products, arithmetic and copies ran while one was open for 12% of the time, Pallas kernels for 0%

profile of v1, /device:TPU:0, one launch (start us, length us, event | category | flops | bytes accessed | tf_op | source)
XLA Modules:
  0.0 152.2 jit_solution(12872344716657278322)
XLA Ops:
  6.5 1.3 collective-permute-start
  7.9 0.7 convert_bitcast_fusion
  9.2 0.7 reduce_sum.38
  9.9 3.5 %collective-permute-done = bf16[1,3,3072]{2,1,0:T(4,128)(2,1)S(1)} collective-permute-done((bf16[1,3,3072]{2,1,0:T(4,128)(2,1)}, bf16[1,3,3072]{2,1,0:T(4,128)(2,1)S(1)}, u32[]{:S(2)}, u32[]{:S(2)}) %collective-permute-start) | collective-permute-done | bytes 18464 | tf_op jit(solution)/shard_map/ppermute | solution.py:13
  13.5 0.9 multiply_reduce_fusion.1
  14.4 0.1 constant_dynamic-update-slice_fusion.126
  14.9 0.1 constant_dynamic-update-slice_fusion.122
  15.0 0.1 constant_dynamic-update-slice_fusion.121
  15.1 0.1 constant_dynamic-update-slice_fusion.120
  15.3 0.1 constant_dynamic-update-slice_fusion.118
  15.4 0.1 constant_dynamic-update-slice_fusion.117
  15.9 0.1 constant_dynamic-update-slice_fusion.112
  16.1 0.1 constant_dynamic-update-slice_fusion.111
  16.4 0.1 constant_dynamic-update-slice_fusion.108
  16.8 0.1 constant_dynamic-update-slice_fusion.104
  16.9 0.1 constant_dynamic-update-slice_fusion.103
  17.7 0.1 constant_dynamic-update-slice_fusion.96
  17.8 0.1 constant_dynamic-update-slice_fusion.95
  18.0 0.1 constant_dynamic-update-slice_fusion.93
  18.3 0.1 constant_dynamic-update-slice_fusion.90
  18.9 0.1 constant_dynamic-update-slice_fusion.85
  19.2 0.1 constant_dynamic-update-slice_fusion.82
  19.4 0.1 constant_dynamic-update-slice_fusion.80
  19.8 0.1 constant_dynamic-update-slice_fusion.76
  20.3 0.1 constant_dynamic-update-slice_fusion.72
  21.1 0.1 constant_dynamic-update-slice_fusion.64
  21.2 0.1 constant_dynamic-update-slice_fusion.63
  21.8 0.1 constant_dynamic-update-slice_fusion.58
  22.1 0.1 constant_dynamic-update-slice_fusion.55
  22.3 0.1 constant_dynamic-update-slice_fusion.53
  22.6 0.1 constant_dynamic-update-slice_fusion.50
  22.8 0.1 constant_dynamic-update-slice_fusion.48
  24.6 0.1 constant_dynamic-update-slice_fusion.32
  26.3 0.1 constant_dynamic-update-slice_fusion.16
  28.0 0.1 constant_dynamic-update-slice_fusion
  28.1 2.2 %copy.141 = bf16[3,128,4992]{2,1,0:T(8,128)(2,1)} copy(bf16[3,128,4992]{2,0,1:T(4,128)(2,1)S(1)} %constant_dynamic-update-slice_fusion) | data formatting | bytes 7667712 | tf_op jit(solution)/shard_map/stack | solution.py:39
  30.4 0.2 fusion.4
  30.6 18.2 %all-gather.4.cloned.1.call-done = bf16[128,1,3,2048]{3,0,2,1:T(8,128)(2,1)} async-done(((bf16[32,1,3,2048]{3,0,2,1:T(8,128)(2,1)}), bf16[128,1,3,2048]{3,0,2,1:T(8,128)(2,1)}) %all-gather.4.cloned.1.call-update) | async-done | bytes 1572880 | tf_op jit(solution)/shard_map/all_gather | solution.py:80
  48.9 1.9 %copy.139 = bf16[128,1,3,2048]{0,3,2,1:T(8,128)(2,1)S(1)} copy(bf16[128,1,3,2048]{3,0,2,1:T(8,128)(2,1)} %all-gather.4.cloned.1.call-done) | data formatting | bytes 3145728 | tf_op jit(solution)/shard_map/all_gather | solution.py:80
  50.8 0.2 multiply_bitcast_fusion
  51.0 1.3 copy.140
  52.3 40.8 %while.14 = (s32[]{:T(128)}, f32[128,3072]{1,0:T(8,128)S(1)}, bf16[128,16,384]{0,2,1:T(8,128)(2,1)}, bf16[384,4992]{1,0:T(8,128)(2,1)}, s32[]{:T(128)}, /*index=5*/s32[]{:T(128)}, s32[]{:T(128)}, s32[]{:T(128)}) while((s32[]{:T(128)}, f32[128,3072]{1,0:T(8,128)S(1)}, bf16[128,16,384]{0,2,1:T(8,128)(2,1)}, ...), condition=%wide.region_1.0_spmd.clone, body=%wide.region_0.0_spmd.clone.sunk | while | flops 302776320 | bytes 5603985 | solution.py:55
  52.3 2.6 %convolution_add_fusion.2 = f32[128,3072]{1,0:T(8,128)S(1)} fusion(bf16[384,4992]{1,0:T(8,128)(2,1)} %get-tuple-element.168, s32[]{:T(128)S(6)} %select_n.34, f32[128,3072]{1,0:T(8,128)S(1)} %get-tuple-element.158, pred[]{:T(512)S(6)} %compare.3, bf16[128,16,384]{0,2,1:T(8,128)(2,1)} %get-tuple-element.167, s32[]{:T(128)} %get-tuple-element.157), kind=kOutput, calls=%fused_computation.clone.1 | convolution fusion | flops 302776320 | bytes 5603845 | tf_op jit(solution)/shard_map/while/body/eval_jaxpr/dot_general | solution.py:53
  54.9 2.5 %convolution_add_fusion.2 = f32[128,3072]{1,0:T(8,128)S(1)} fusion(bf16[384,4992]{1,0:T(8,128)(2,1)} %get-tuple-element.168, s32[]{:T(128)S(6)} %select_n.34, f32[128,3072]{1,0:T(8,128)S(1)} %get-tuple-element.158, pred[]{:T(512)S(6)} %compare.3, bf16[128,16,384]{0,2,1:T(8,128)(2,1)} %get-tuple-element.167, s32[]{:T(128)} %get-tuple-element.157), kind=kOutput, calls=%fused_computation.clone.1 | convolution fusion | flops 302776320 | bytes 5603845 | tf_op jit(solution)/shard_map/while/body/eval_jaxpr/dot_general | solution.py:53
  57.5 2.5 %convolution_add_fusion.2 = f32[128,3072]{1,0:T(8,128)S(1)} fusion(bf16[384,4992]{1,0:T(8,128)(2,1)} %get-tuple-element.168, s32[]{:T(128)S(6)} %select_n.34, f32[128,3072]{1,0:T(8,128)S(1)} %get-tuple-element.158, pred[]{:T(512)S(6)} %compare.3, bf16[128,16,384]{0,2,1:T(8,128)(2,1)} %get-tuple-element.167, s32[]{:T(128)} %get-tuple-element.157), kind=kOutput, calls=%fused_computation.clone.1 | convolution fusion | flops 302776320 | bytes 5603845 | tf_op jit(solution)/shard_map/while/body/eval_jaxpr/dot_general | solution.py:53
  60.0 2.5 %convolution_add_fusion.2 = f32[128,3072]{1,0:T(8,128)S(1)} fusion(bf16[384,4992]{1,0:T(8,128)(2,1)} %get-tuple-element.168, s32[]{:T(128)S(6)} %select_n.34, f32[128,3072]{1,0:T(8,128)S(1)} %get-tuple-element.158, pred[]{:T(512)S(6)} %compare.3, bf16[128,16,384]{0,2,1:T(8,128)(2,1)} %get-tuple-element.167, s32[]{:T(128)} %get-tuple-element.157), kind=kOutput, calls=%fused_computation.clone.1 | convolution fusion | flops 302776320 | bytes 5603845 | tf_op jit(solution)/shard_map/while/body/eval_jaxpr/dot_general | solution.py:53
  62.6 2.5 %convolution_add_fusion.2 = f32[128,3072]{1,0:T(8,128)S(1)} fusion(bf16[384,4992]{1,0:T(8,128)(2,1)} %get-tuple-element.168, s32[]{:T(128)S(6)} %select_n.34, f32[128,3072]{1,0:T(8,128)S(1)} %get-tuple-element.158, pred[]{:T(512)S(6)} %compare.3, bf16[128,16,384]{0,2,1:T(8,128)(2,1)} %get-tuple-element.167, s32[]{:T(128)} %get-tuple-element.157), kind=kOutput, calls=%fused_computation.clone.1 | convolution fusion | flops 302776320 | bytes 5603845 | tf_op jit(solution)/shard_map/while/body/eval_jaxpr/dot_general | solution.py:53
  65.1 2.5 %convolution_add_fusion.2 = f32[128,3072]{1,0:T(8,128)S(1)} fusion(bf16[384,4992]{1,0:T(8,128)(2,1)} %get-tuple-element.168, s32[]{:T(128)S(6)} %select_n.34, f32[128,3072]{1,0:T(8,128)S(1)} %get-tuple-element.158, pred[]{:T(512)S(6)} %compare.3, bf16[128,16,384]{0,2,1:T(8,128)(2,1)} %get-tuple-element.167, s32[]{:T(128)} %get-tuple-element.157), kind=kOutput, calls=%fused_computation.clone.1 | convolution fusion | flops 302776320 | bytes 5603845 | tf_op jit(solution)/shard_map/while/body/eval_jaxpr/dot_general | solution.py:53
  67.7 2.5 %convolution_add_fusion.2 = f32[128,3072]{1,0:T(8,128)S(1)} fusion(bf16[384,4992]{1,0:T(8,128)(2,1)} %get-tuple-element.168, s32[]{:T(128)S(6)} %select_n.34, f32[128,3072]{1,0:T(8,128)S(1)} %get-tuple-element.158, pred[]{:T(512)S(6)} %compare.3, bf16[128,16,384]{0,2,1:T(8,128)(2,1)} %get-tuple-element.167, s32[]{:T(128)} %get-tuple-element.157), kind=kOutput, calls=%fused_computation.clone.1 | convolution fusion | flops 302776320 | bytes 5603845 | tf_op jit(solution)/shard_map/while/body/eval_jaxpr/dot_general | solution.py:53
  70.2 2.5 %convolution_add_fusion.2 = f32[128,3072]{1,0:T(8,128)S(1)} fusion(bf16[384,4992]{1,0:T(8,128)(2,1)} %get-tuple-element.168, s32[]{:T(128)S(6)} %select_n.34, f32[128,3072]{1,0:T(8,128)S(1)} %get-tuple-element.158, pred[]{:T(512)S(6)} %compare.3, bf16[128,16,384]{0,2,1:T(8,128)(2,1)} %get-tuple-element.167, s32[]{:T(128)} %get-tuple-element.157), kind=kOutput, calls=%fused_computation.clone.1 | convolution fusion | flops 302776320 | bytes 5603845 | tf_op jit(solution)/shard_map/while/body/eval_jaxpr/dot_general | solution.py:53
  72.7 2.5 %convolution_add_fusion.2 = f32[128,3072]{1,0:T(8,128)S(1)} fusion(bf16[384,4992]{1,0:T(8,128)(2,1)} %get-tuple-element.168, s32[]{:T(128)S(6)} %select_n.34, f32[128,3072]{1,0:T(8,128)S(1)} %get-tuple-element.158, pred[]{:T(512)S(6)} %compare.3, bf16[128,16,384]{0,2,1:T(8,128)(2,1)} %get-tuple-element.167, s32[]{:T(128)} %get-tuple-element.157), kind=kOutput, calls=%fused_computation.clone.1 | convolution fusion | flops 302776320 | bytes 5603845 | tf_op jit(solution)/shard_map/while/body/eval_jaxpr/dot_general | solution.py:53
  75.3 2.5 %convolution_add_fusion.2 = f32[128,3072]{1,0:T(8,128)S(1)} fusion(bf16[384,4992]{1,0:T(8,128)(2,1)} %get-tuple-element.168, s32[]{:T(128)S(6)} %select_n.34, f32[128,3072]{1,0:T(8,128)S(1)} %get-tuple-element.158, pred[]{:T(512)S(6)} %compare.3, bf16[128,16,384]{0,2,1:T(8,128)(2,1)} %get-tuple-element.167, s32[]{:T(128)} %get-tuple-element.157), kind=kOutput, calls=%fused_computation.clone.1 | convolution fusion | flops 302776320 | bytes 5603845 | tf_op jit(solution)/shard_map/while/body/eval_jaxpr/dot_general | solution.py:53
  77.8 2.5 %convolution_add_fusion.2 = f32[128,3072]{1,0:T(8,128)S(1)} fusion(bf16[384,4992]{1,0:T(8,128)(2,1)} %get-tuple-element.168, s32[]{:T(128)S(6)} %select_n.34, f32[128,3072]{1,0:T(8,128)S(1)} %get-tuple-element.158, pred[]{:T(512)S(6)} %compare.3, bf16[128,16,384]{0,2,1:T(8,128)(2,1)} %get-tuple-element.167, s32[]{:T(128)} %get-tuple-element.157), kind=kOutput, calls=%fused_computation.clone.1 | convolution fusion | flops 302776320 | bytes 5603845 | tf_op jit(solution)/shard_map/while/body/eval_jaxpr/dot_general | solution.py:53
  80.4 2.5 %convolution_add_fusion.2 = f32[128,3072]{1,0:T(8,128)S(1)} fusion(bf16[384,4992]{1,0:T(8,128)(2,1)} %get-tuple-element.168, s32[]{:T(128)S(6)} %select_n.34, f32[128,3072]{1,0:T(8,128)S(1)} %get-tuple-element.158, pred[]{:T(512)S(6)} %compare.3, bf16[128,16,384]{0,2,1:T(8,128)(2,1)} %get-tuple-element.167, s32[]{:T(128)} %get-tuple-element.157), kind=kOutput, calls=%fused_computation.clone.1 | convolution fusion | flops 302776320 | bytes 5603845 | tf_op jit(solution)/shard_map/while/body/eval_jaxpr/dot_general | solution.py:53
  82.9 2.5 %convolution_add_fusion.2 = f32[128,3072]{1,0:T(8,128)S(1)} fusion(bf16[384,4992]{1,0:T(8,128)(2,1)} %get-tuple-element.168, s32[]{:T(128)S(6)} %select_n.34, f32[128,3072]{1,0:T(8,128)S(1)} %get-tuple-element.158, pred[]{:T(512)S(6)} %compare.3, bf16[128,16,384]{0,2,1:T(8,128)(2,1)} %get-tuple-element.167, s32[]{:T(128)} %get-tuple-element.157), kind=kOutput, calls=%fused_computation.clone.1 | convolution fusion | flops 302776320 | bytes 5603845 | tf_op jit(solution)/shard_map/while/body/eval_jaxpr/dot_general | solution.py:53
  85.5 2.5 %convolution_add_fusion.2 = f32[128,3072]{1,0:T(8,128)S(1)} fusion(bf16[384,4992]{1,0:T(8,128)(2,1)} %get-tuple-element.168, s32[]{:T(128)S(6)} %select_n.34, f32[128,3072]{1,0:T(8,128)S(1)} %get-tuple-element.158, pred[]{:T(512)S(6)} %compare.3, bf16[128,16,384]{0,2,1:T(8,128)(2,1)} %get-tuple-element.167, s32[]{:T(128)} %get-tuple-element.157), kind=kOutput, calls=%fused_computation.clone.1 | convolution fusion | flops 302776320 | bytes 5603845 | tf_op jit(solution)/shard_map/while/body/eval_jaxpr/dot_general | solution.py:53
  88.0 2.5 %convolution_add_fusion.2 = f32[128,3072]{1,0:T(8,128)S(1)} fusion(bf16[384,4992]{1,0:T(8,128)(2,1)} %get-tuple-element.168, s32[]{:T(128)S(6)} %select_n.34, f32[128,3072]{1,0:T(8,128)S(1)} %get-tuple-element.158, pred[]{:T(512)S(6)} %compare.3, bf16[128,16,384]{0,2,1:T(8,128)(2,1)} %get-tuple-element.167, s32[]{:T(128)} %get-tuple-element.157), kind=kOutput, calls=%fused_computation.clone.1 | convolution fusion | flops 302776320 | bytes 5603845 | tf_op jit(solution)/shard_map/while/body/eval_jaxpr/dot_general | solution.py:53
  90.5 2.5 %convolution_add_fusion.2 = f32[128,3072]{1,0:T(8,128)S(1)} fusion(bf16[384,4992]{1,0:T(8,128)(2,1)} %get-tuple-element.168, s32[]{:T(128)S(6)} %select_n.34, f32[128,3072]{1,0:T(8,128)S(1)} %get-tuple-element.158, pred[]{:T(512)S(6)} %compare.3, bf16[128,16,384]{0,2,1:T(8,128)(2,1)} %get-tuple-element.167, s32[]{:T(128)} %get-tuple-element.157), kind=kOutput, calls=%fused_computation.clone.1 | convolution fusion | flops 302776320 | bytes 5603845 | tf_op jit(solution)/shard_map/while/body/eval_jaxpr/dot_general | solution.py:53
  93.1 0.6 multiply_reduce_fusion
  93.6 0.7 fusion.29
  94.3 1.4 multiply_multiply_fusion
  95.8 45.4 %all-gather.6.cloned.1.call-done = f32[512,3072]{1,0:T(8,128)} async-done(((f32[128,3072]{1,0:T(8,128)}), f32[512,3072]{1,0:T(8,128)}) %all-gather.6.cloned.1.call-update) | async-done | bytes 6291472 | tf_op jit(solution)/shard_map/all_gather | solution.py:92
  141.2 3.4 %reduce_sum.39 = f32[128,3072]{1,0:T(8,128)S(1)} reduce(f32[4,128,3072]{2,1,0:T(8,128)} %bitcast.560, f32[]{:T(128)} %constant.62.clone.1), dimensions={0}, to_apply=%region_5.6 | reduce | flops 1179648 | bytes 7864324 | tf_op jit(solution)/shard_map/reduce_sum | solution.py:93
  144.6 0.8 constant_dynamic-slice_fusion
  (107 shorter events, 10.2 us)
Async XLA Ops:
  6.5 42.3 %all-gather.4.cloned.1.call-start = ((), (), s32[]{:S(2)}) async-start(), calls=%async_computation | async-start | bytes 1966080 | tf_op jit(solution)/shard_map/all_gather | solution.py:80
  6.5 6.9 %collective-permute-start = (bf16[1,3,3072]{2,1,0:T(4,128)(2,1)}, bf16[1,3,3072]{2,1,0:T(4,128)(2,1)S(1)}, u32[]{:S(2)}, u32[]{:S(2)}) collective-permute-start(bf16[1,3,3072]{2,1,0:T(4,128)(2,1)} %param.7), channel_id=1, source_target_pairs={{1,0},{2,1},{3,2},{5,4},{6,5},{7,6},{9,8},{10,9},{11,10},{13,12},{... | collective-permute-start | bytes 55304 | tf_op jit(solution)/shard_map/ppermute | solution.py:13
  7.8 133.3 %all-gather.6.cloned.1.call-start = ((), (), s32[]{:S(2)}) async-start(), calls=%async_computation.1 | async-start | bytes 7864320 | tf_op jit(solution)/shard_map/all_gather | solution.py:92
  52.3 40.8 %copy-start = (bf16[128,1,3,2048]{3,0,2,1:T(8,128)(2,1)S(1)}, bf16[128,1,3,2048]{3,0,2,1:T(8,128)(2,1)}, u32[]{:S(2)}) copy-start(bf16[128,1,3,2048]{3,0,2,1:T(8,128)(2,1)} %all-gather.4.cloned.1.call-done) | copy-start | bytes 4718596
Sparse Core Ops, SparseCore 0:
  8.9 39.9 all-gather.3
  95.9 45.2 all-gather.5
